TPU v7x, 256 devices: a whole 4x4x8 slice. The times are simulated.
256 devices in a mesh: dp: 4 (over y), mp: 64 (over x, z, core).
Axes of the slice: x: 4, y: 4, z: 8, core: 2. Of those that a mesh axis runs over, the one named last changes fastest.
Arguments:
- inputs: bfloat16 [8, 256, 6144], P('dp', None, 'mp'), may hold values from -6 to 6
- cotangent: bfloat16 [8, 256, 6144], P('dp', None, 'mp'), may hold values from -6 to 6
- w_up: bfloat16 [6144, 24576], P('dp', 'mp'), may hold values from -0.078125 to 0.078125
- w_down: bfloat16 [24576, 6144], P('mp', 'dp'), may hold values from -0.0390625 to 0.0390625
- thresholds: float32 [2], replicated, may hold values from 23592.96 to 58982.4
Outputs:
- grad_up: float32 [6144, 24576], P('dp', 'mp')
- grad_down: float32 [24576, 6144], P('mp', 'dp')
- norms: float32 [8, 2], P('dp')
All inputs are finite; a program needn't handle non-finite values.
Results may differ from a plain program's by a relative error of at most 0.0085.
Values may be sent and summed in bfloat16 or wider, within the bound.
A program may use at most 128 MiB of HBM per device.

v0:
```python
import jax
import jax.numpy as jnp
from jax import lax
from jax.sharding import PartitionSpec as P

inv_root_two = 0.7071067811865476
inv_root_two_pi = 0.3989422804014327


def sent_to_all(shard, axis):
    copies = jnp.broadcast_to(shard, (lax.axis_size(axis), *shard.shape))
    return lax.all_to_all(copies, axis, split_axis=0, concat_axis=0, tiled=True)


def taken_together(shard, axis):
    return sent_to_all(shard, axis).sum(axis=0)


def packed_total(arrays, axis):
    line, at, outs = (jnp.concatenate([a.reshape(-1) for a in arrays]), 0, [])
    running = taken_together(line, axis)
    for a in arrays:
        outs.append(running[at : at + a.size].reshape(a.shape))
        at += a.size
    return tuple(outs)


def split_up(shard, dim, count):
    shape = shard.shape
    pieces = shard.reshape(*shape[:dim], count, shape[dim] // count, *shape[dim + 1 :])
    return jnp.moveaxis(pieces, dim, 0)


def sum_at_owner(shard, axis, dim):
    pieces = split_up(shard, dim, lax.axis_size(axis))
    arrived = lax.all_to_all(pieces, axis, split_axis=0, concat_axis=0, tiled=True)
    return arrived.astype(jnp.float32).sum(axis=0)


def normal_cdf(value):
    return 0.5 * (1.0 + lax.erf(value * inv_root_two))


def gram_of(array, images, patches):
    cube = array.reshape(images, patches, -1)
    return jnp.einsum("btd,bsd->bts", cube, cube, preferred_element_type=jnp.float32)


def on_device(inputs, cotangent, w_up, w_down, thresholds):
    images, patches, local_feats = inputs.shape
    count_rows = images * patches
    x_whole = lax.all_gather(inputs, "mp", axis=2, tiled=True).reshape(count_rows, -1)
    hidden_local = w_up.shape[1]
    columns = x_whole
    pre = jnp.dot(
        columns, lax.all_gather(w_up, "dp", axis=0, tiled=True), preferred_element_type=jnp.float32
    )
    act = (pre * normal_cdf(pre)).astype(jnp.bfloat16)
    dy_whole = lax.all_gather(cotangent, "mp", axis=2, tiled=True).reshape(count_rows, -1)
    columns = dy_whole
    dact = lax.dot_general(
        columns,
        lax.all_gather(w_down, "dp", axis=1, tiled=True),
        (((1,), (1,)), ((), ())),
        preferred_element_type=jnp.float32,
    )
    slope = normal_cdf(pre) + pre * jnp.exp(-0.5 * pre * pre) * inv_root_two_pi
    dpre = (dact * slope).astype(jnp.bfloat16)
    gram_dpre = gram_of(dpre, images, patches)
    gram_act = gram_of(act, images, patches)
    part_up = jnp.sum(gram_of(x_whole, images, patches) * gram_dpre, axis=(1, 2))
    part_down = jnp.sum(gram_act * gram_of(dy_whole, images, patches), axis=(1, 2))
    sq_up, sq_down = packed_total((part_up, part_down), "mp")
    norms = jnp.stack([jnp.sqrt(sq_up), jnp.sqrt(sq_down)], axis=1)
    factor = jnp.minimum(1.0, thresholds[None, :] / (norms + 1e-06))
    dpre_clip = (
        (
            factor[:, 0][:, None, None]
            * dpre.reshape(images, patches, hidden_local).astype(jnp.float32)
        )
        .astype(jnp.bfloat16)
        .reshape(count_rows, hidden_local)
    )
    cot_clip = (
        (factor[:, 1][:, None, None] * dy_whole.reshape(images, patches, -1).astype(jnp.float32))
        .astype(jnp.bfloat16)
        .reshape(count_rows, -1)
    )
    columns = x_whole
    grad_up = lax.psum_scatter(
        lax.dot_general(
            columns, dpre_clip, (((0,), (0,)), ((), ())), preferred_element_type=jnp.float32
        ).astype(jnp.bfloat16),
        "dp",
        scatter_dimension=0,
        tiled=True,
    ).astype(jnp.float32)
    down_full = lax.dot_general(
        act, cot_clip, (((0,), (0,)), ((), ())), preferred_element_type=jnp.float32
    )
    grad_down = sum_at_owner(down_full.astype(jnp.bfloat16), "dp", 1)
    return (grad_up, grad_down, norms)


def solution(mesh):
    in_specs = (P("dp", None, "mp"), P("dp", None, "mp"), P("dp", "mp"), P("mp", "dp"), P())
    out_specs = (P("dp", "mp"), P("mp", "dp"), P("dp", None))
    return jax.shard_map(
        on_device, mesh=mesh, in_specs=in_specs, out_specs=out_specs, check_vma=False
    )
```

profile of v0, /device:TPU:1, one launch (start us, length us, event | category | flops | bytes accessed | tf_op | source)
XLA Modules:
  0.0 445.1 jit_solution(11769768210793305239)
XLA Ops:
  7.2 0.7 all-gather.5.cloned.1.call-update
  7.9 0.7 all-gather.7.cloned.1.call-update
  8.7 0.7 all-gather.11.cloned.1.call-update
  10.0 85.6 %all-gather.5.cloned.1.call-done = bf16[2,256,6144]{1,2,0:T(8,128)(2,1)} async-done(((bf16[2,256,96]{1,2,0:T(8,128)(2,1)}), bf16[2,256,6144]{1,2,0:T(8,128)(2,1)}) %all-gather.5.cloned.1.call-update) | async-done | bytes 6291472 | tf_op jit(solution)/shard_map/all_gather | solution.py:52
  95.5 8.7 %copy.32 = bf16[2,256,6144]{2,1,0:T(8,128)(2,1)} copy(bf16[2,256,6144]{1,2,0:T(8,128)(2,1)} %all-gather.5.cloned.1.call-done) | data formatting | bytes 12582912 | tf_op jit(solution)/shard_map/all_gather | solution.py:52
  104.2 71.4 %all-gather.7.cloned.1.call-done = bf16[2,256,6144]{1,2,0:T(8,128)(2,1)} async-done(((bf16[2,256,96]{1,2,0:T(8,128)(2,1)}), bf16[2,256,6144]{1,2,0:T(8,128)(2,1)}) %all-gather.7.cloned.1.call-update) | async-done | bytes 6291472 | tf_op jit(solution)/shard_map/all_gather | solution.py:59
  175.6 8.7 %copy.31 = bf16[2,256,6144]{2,1,0:T(8,128)(2,1)} copy(bf16[2,256,6144]{1,2,0:T(8,128)(2,1)} %all-gather.7.cloned.1.call-done) | data formatting | bytes 12582912 | tf_op jit(solution)/shard_map/all_gather | solution.py:59
  184.3 44.5 %all-gather.11.cloned.1.call-done = bf16[6144,384]{1,0:T(8,128)(2,1)} async-done(((bf16[1536,384]{1,0:T(8,128)(2,1)}), bf16[6144,384]{1,0:T(8,128)(2,1)}) %all-gather.11.cloned.1.call-update) | async-done | bytes 4718608 | tf_op jit(solution)/shard_map/all_gather | solution.py:56
  228.8 7.0 %multiply_convert_fusion.2 = (bf16[512,384]{1,0:T(8,128)(2,1)S(1)}, f32[512,384]{1,0:T(8,128)S(1)}) fusion(bf16[512,6144]{1,0:T(8,128)(2,1)} %bitcast.47, bf16[6144,384]{1,0:T(8,128)(2,1)} %all-gather.11.cloned.1.call-done), kind=kOutput, calls=%fused_computation.18 | convolution fusion | flops 2416902144 | bytes 12189696 | tf_op jit(solution)/shard_map/dot_general | solution.py:55
  235.7 50.3 %all-gather.9.cloned.1.call-done = bf16[384,6144]{1,0:T(8,128)(2,1)} async-done(((bf16[384,1536]{1,0:T(8,128)(2,1)}), bf16[384,6144]{1,0:T(8,128)(2,1)}) %all-gather.9.cloned.1.call-update) | async-done | bytes 4718608 | tf_op jit(solution)/shard_map/all_gather | solution.py:63
  286.0 7.7 %fusion.1 = bf16[512,384]{1,0:T(8,128)(2,1)S(1)} fusion(bf16[512,6144]{1,0:T(8,128)(2,1)} %bitcast.46, bf16[384,6144]{1,0:T(8,128)(2,1)} %all-gather.9.cloned.1.call-done, f32[512,384]{1,0:T(8,128)S(1)} %get-tuple-element.25), kind=kOutput, calls=%fused_computation.7 | convolution fusion | flops 2417885184 | bytes 12189696 | tf_op jit(solution)/shard_map/dot_general | solution.py:61
  294.4 7.4 %fusion.2 = f32[2]{0:T(128)S(1)} fusion(f32[2,256,256]{2,1,0:T(8,128)S(1)} %fusion.9, bf16[2,256,6144]{1,2,0:T(8,128)(2,1)} %all-gather.5.cloned.1.call-done), kind=kOutput, calls=%fused_computation.11 | convolution fusion | flops 1610874880 | bytes 6815752 | tf_op jit(solution)/shard_map/btd,bsd->bts/dot_general | solution.py:46
  301.8 2.7 fusion.3
  305.2 10.8 %all-to-all-start = ((f32[64,1,4]{2,1,0:T(1,128)}), f32[64,1,4]{2,1,0:T(1,128)S(1)}, u32[]{:S(2)}, u32[]{:S(2)}) async-start(f32[64,1,4]{2,1,0:T(1,128)} %broadcast_in_dim.4), calls=%async_computation | async-start | bytes 65536 | tf_op jit(solution)/shard_map/all_to_all | solution.py:12
  316.5 8.8 %all-to-all-done = f32[64,1,4]{2,1,0:T(1,128)S(1)} async-done(((f32[64,1,4]{2,1,0:T(1,128)}), f32[64,1,4]{2,1,0:T(1,128)S(1)}, u32[]{:S(2)}, u32[]{:S(2)}) %all-to-all-start) | async-done | bytes 1056 | tf_op jit(solution)/shard_map/all_to_all | solution.py:12
  325.5 8.6 %fusion = bf16[6144,384]{0,1:T(8,128)(2,1)} fusion(bf16[2,256,6144]{1,2,0:T(8,128)(2,1)} %all-gather.5.cloned.1.call-done, bf16[2,256,384]{1,2,0:T(8,128)(2,1)S(1)} %copy.34, f32[2]{0:T(128)S(1)} %get-tuple-element.21), kind=kOutput, calls=%fused_computation.4 | convolution fusion | flops 2418868224 | bytes 11403272 | tf_op jit(solution)/shard_map/dot_general | solution.py:91
  334.2 7.5 %multiply_convert_fusion = bf16[2,256,6144]{1,2,0:T(8,128)(2,1)} fusion(bf16[2,256,6144]{1,2,0:T(8,128)(2,1)} %all-gather.7.cloned.1.call-done, f32[2]{0:T(128)S(1)} %get-tuple-element.20), kind=kLoop, calls=%fused_computation | loop fusion | flops 9437184 | bytes 12582920 | tf_op jit(solution)/shard_map/convert_element_type | solution.py:86
  341.7 8.7 %copy.35 = bf16[2,256,6144]{2,1,0:T(8,128)(2,1)} copy(bf16[2,256,6144]{1,2,0:T(8,128)(2,1)} %multiply_convert_fusion) | data formatting | bytes 12582912 | tf_op jit(solution)/shard_map/convert_element_type | solution.py:86
  350.4 5.4 %convolution_convert_fusion = bf16[384,6144]{1,0:T(8,128)(2,1)S(1)} fusion(bf16[512,384]{1,0:T(8,128)(2,1)S(1)} %get-tuple-element.24, bf16[512,6144]{1,0:T(8,128)(2,1)} %bitcast.43), kind=kOutput, calls=%fused_computation.3 | convolution fusion | flops 2418278400 | bytes 11403264 | tf_op jit(solution)/shard_map/dot_general | solution.py:98
  355.8 2.6 copy.44
  358.4 4.9 %all-to-all-start.1 = ((bf16[4,384,1536]{2,1,0:T(8,128)(2,1)}), bf16[4,384,1536]{2,1,0:T(8,128)(2,1)}, u32[]{:S(2)}, u32[]{:S(2)}) async-start(bf16[4,384,1536]{2,1,0:T(8,128)(2,1)} %bitcast.44), calls=%async_computation.2 | async-start | bytes 9437184 | tf_op jit(solution)/shard_map/all_to_all | solution.py:36
  364.0 67.2 %all-to-all-done.1 = bf16[4,384,1536]{2,1,0:T(8,128)(2,1)} async-done(((bf16[4,384,1536]{2,1,0:T(8,128)(2,1)}), bf16[4,384,1536]{2,1,0:T(8,128)(2,1)}, u32[]{:S(2)}, u32[]{:S(2)}) %all-to-all-start.1) | async-done | bytes 4718624 | tf_op jit(solution)/shard_map/all_to_all | solution.py:36
  431.2 4.7 %convert_reduce_fusion = f32[384,1536]{1,0:T(8,128)} fusion(bf16[4,384,1536]{2,1,0:T(8,128)(2,1)} %all-to-all-done.1), kind=kLoop, calls=%fused_computation.2 | loop fusion | flops 4128768 | bytes 7077888 | tf_op jit(solution)/shard_map/reduce_sum | solution.py:37
  435.9 2.7 copy.37
  (25 shorter events, 3.4 us)
Async XLA Ops:
  7.2 88.4 %all-gather.5.cloned.1.call-start = ((), (), s32[]{:S(2)}) async-start(), calls=%async_computation.3 | async-start | bytes 6389760 | tf_op jit(solution)/shard_map/all_gather | solution.py:52
  7.9 167.7 %all-gather.7.cloned.1.call-start = ((), (), s32[]{:S(2)}) async-start(), calls=%async_computation.4 | async-start | bytes 6389760 | tf_op jit(solution)/shard_map/all_gather | solution.py:59
  8.6 220.1 %all-gather.11.cloned.1.call-start = ((), (), s32[]{:S(2)}) async-start(), calls=%async_computation.6 | async-start | bytes 5898240 | tf_op jit(solution)/shard_map/all_gather | solution.py:56
  9.4 276.6 %all-gather.9.cloned.1.call-start = ((), (), s32[]{:S(2)}) async-start(), calls=%async_computation.5 | async-start | bytes 5898240 | tf_op jit(solution)/shard_map/all_gather | solution.py:63
  294.0 7.8 %slice-start = ((s8[6291456]{0:T(1024)(128)(4,1)}), s8[4194304]{0:T(1024)(128)(4,1)S(1)}, s32[]{:S(2)}) async-start(s8[6291456]{0:T(1024)(128)(4,1)} %bitcast.41), calls=%async_computation.8 | async-start | bytes 8388608
  294.4 7.4 %slice-start.1 = ((s8[6291456]{0:T(1024)(128)(4,1)}), s8[2097152]{0:T(1024)(128)(4,1)S(1)}, s32[]{:S(2)}) async-start(s8[6291456]{0:T(1024)(128)(4,1)} %bitcast.41), calls=%async_computation.9 | async-start | bytes 4194304
  301.8 23.7 %copy-start = (f32[2]{0:T(128)S(1)}, f32[2]{0:T(128)}, u32[]{:S(2)}) copy-start(f32[2]{0:T(128)} %param.9) | copy-start | bytes 28
  305.2 20.1 %all-to-all-start = ((f32[64,1,4]{2,1,0:T(1,128)}), f32[64,1,4]{2,1,0:T(1,128)S(1)}, u32[]{:S(2)}, u32[]{:S(2)}) async-start(f32[64,1,4]{2,1,0:T(1,128)} %broadcast_in_dim.4), calls=%async_computation | async-start | bytes 65536 | tf_op jit(solution)/shard_map/all_to_all | solution.py:12
  316.1 119.8 %reduce-scatter.2.cloned.1.call-start = ((), (), s32[]{:S(2)}) async-start(), calls=%async_computation.7 | async-start | bytes 5898240 | tf_op jit(solution)/shard_map/reduce_scatter | solution.py:90
  358.4 72.8 %all-to-all-start.1 = ((bf16[4,384,1536]{2,1,0:T(8,128)(2,1)}), bf16[4,384,1536]{2,1,0:T(8,128)(2,1)}, u32[]{:S(2)}, u32[]{:S(2)}) async-start(bf16[4,384,1536]{2,1,0:T(8,128)(2,1)} %bitcast.44), calls=%async_computation.2 | async-start | bytes 9437184 | tf_op jit(solution)/shard_map/all_to_all | solution.py:36
Sparse Core Ops, SparseCore 0:
  10.8 84.6 all-gather.4
  98.3 77.2 all-gather.6
  177.4 51.2 all-gather.10
  230.4 55.5 all-gather.8
  334.3 59.8 reduce-scatter.1
where the time goes:
time: 446 us; the launch traced here: 445 us
  waiting for transfers between devices  330 us (74%)
  matrix products  39.5 us (9%)
  local copies, waits for them, and re-layouts  32.9 us (7%)
  starting transfers between devices  16.1 us (4%)
  between operations  13.9 us (3%)
  other arithmetic  12.4 us (3%)
    all_gather x1, waiting for transfers between devices, on_device(): lax.all_gather(inputs, 'mp', axis=2, tiled=True).reshape(count_rows, -1)  85.6 us
    all_gather x1, waiting for transfers between devices, on_device(): lax.all_gather(cotangent, 'mp', axis=2, tiled=True).reshape(count_rows, -1)  71.4 us
    all_to_all x1, waiting for transfers between devices, sum_at_owner(): lax.all_to_all(pieces, axis, split_axis=0, concat_axis=0, tiled=True)  67.2 us
    all_gather x1, waiting for transfers between devices, on_device(): lax.all_gather(w_down, 'dp', axis=1, tiled=True)  50.3 us
    all_gather x1, waiting for transfers between devices, on_device(): lax.all_gather(w_up, 'dp', axis=0, tiled=True)  44.5 us
    all_to_all x1, starting transfers between devices, sent_to_all(): return lax.all_to_all(copies, axis, split_axis=0, concat_axis=0, tiled=True)  10.8 us
    dot_general x4, matrix products, gram_of(): jnp.einsum('btd,bsd->bts', cube, cube, preferred_element_type=jnp.float32)  10.8 us
  transfers between devices with their start and end apart: 7, of which 6 were waited for; matrix products, arithmetic and copies ran while one was open for 12% of the time, Pallas kernels for 0%

commit v1 on v0

--- a/solution.py
+++ b/solution.py
@@ -1,3 +1,4 @@
+import functools
 import jax
 import jax.numpy as jnp
 from jax import lax
@@ -5,6 +6,41 @@
 
 inv_root_two = 0.7071067811865476
 inv_root_two_pi = 0.3989422804014327
+
+
+def bring_table_on(local_array, on_dim):
+    local_array = jnp.moveaxis(local_array, 0, on_dim)
+    current_value = local_array.shape
+    return local_array.reshape(
+        *current_value[:on_dim],
+        current_value[on_dim] * current_value[on_dim + 1],
+        *current_value[on_dim + 2 :]
+    )
+
+
+def make_ways_on_mesh(tile_in, axis_key, array_dim):
+    n = lax.axis_size(axis_key)
+    z_new = map(lambda k0: (k0, (k0 + 1) % n), range(n))
+    seen = list(z_new)
+    views = [(dev, pp) for pp, dev in seen]
+    w_next, a_now = ([], [])
+    for m in range(n - 1):
+        if m % 2 == 0:
+            after = lax.ppermute(w_next[-1] if w_next else tile_in, axis_name=axis_key, perm=seen)
+            w_next.append(after)
+        else:
+            a_now.append(
+                lax.ppermute(a_now[-1] if a_now else tile_in, axis_name=axis_key, perm=views)
+            )
+    z1 = jnp.stack([*w_next[::-1], tile_in, *a_now], axis=0)
+    g_now = len(w_next)
+    block_now = lax.axis_index(axis_key)
+    then = block_now - g_now
+    z1 = z1[(jnp.arange(n) - then) % n]
+    return bring_table_on(z1, array_dim)
+
+
+obtain_lanes = functools.partial(make_ways_on_mesh, axis_key="dp", array_dim=1)
 
 
 def sent_to_all(shard, axis):
@@ -59,10 +95,7 @@
     dy_whole = lax.all_gather(cotangent, "mp", axis=2, tiled=True).reshape(count_rows, -1)
     columns = dy_whole
     dact = lax.dot_general(
-        columns,
-        lax.all_gather(w_down, "dp", axis=1, tiled=True),
-        (((1,), (1,)), ((), ())),
-        preferred_element_type=jnp.float32,
+        columns, obtain_lanes(w_down), (((1,), (1,)), ((), ())), preferred_element_type=jnp.float32
     )
     slope = normal_cdf(pre) + pre * jnp.exp(-0.5 * pre * pre) * inv_root_two_pi
     dpre = (dact * slope).astype(jnp.bfloat16)

time: 446 us -> 391 us (0.88)
  waiting for transfers between devices: 330 us -> 250 us
  blocking collectives: 0 us -> 20.2 us
  local copies, waits for them, and re-layouts: 32.9 us -> 44.5 us
  starting transfers between devices: 16.1 us -> 10.3 us
    all_gather x1, waiting for transfers between devices: 85.6 us -> 16.2 us  [on_device(): lax.all_gather(inputs, 'mp', axis=2, tiled=True).reshape(count_rows, -1)]
    all_gather x1 -> x0, waiting for transfers between devices: 50.3 us -> none  [on_device(): lax.all_gather(w_down, 'dp', axis=1, tiled=True)]
    ppermute x0 -> x3, waiting for transfers between devices: none -> 48.7 us  [the longest x2 48.7 us: make_ways_on_mesh(): lax.ppermute(w_next[-1] if w_next else tile_in, axis_name=axis_key, perm=...]
    all_to_all x0 -> x1, blocking collectives: none -> 20.2 us  [sent_to_all(): return lax.all_to_all(copies, axis, split_axis=0, concat_axis=0, tiled=True)]
    all_to_all x1 -> x0, starting transfers between devices: 10.8 us -> none  [sent_to_all(): return lax.all_to_all(copies, axis, split_axis=0, concat_axis=0, tiled=True)]
    all_to_all x1 -> x0, waiting for transfers between devices: 8.83 us -> none  [sent_to_all(): return lax.all_to_all(copies, axis, split_axis=0, concat_axis=0, tiled=True)]
    transpose x0 -> x1, local copies, waits for them, and re-layouts: none -> 6.8 us  [bring_table_on(): local_array = jnp.moveaxis(local_array, 0, on_dim)]
    gather x0 -> x1, local copies, waits for them, and re-layouts: none -> 5.35 us  [make_ways_on_mesh(): z1 = z1[(jnp.arange(n) - then) % n]]
  transfers between devices with their start and end apart: 7 -> 8, of which waited for: 6 -> 6; matrix products, arithmetic and copies ran while one was open for 12% -> 16% of each run, Pallas kernels for 0% -> 0%
where the time goes in v1:
time: 391 us; the launch traced here: 390 us
  waiting for transfers between devices  250 us (64%)
  local copies, waits for them, and re-layouts  44.5 us (11%)
  matrix products  35.1 us (9%)
  blocking collectives  20.2 us (5%)
  other arithmetic  16.1 us (4%)
  between operations  13.9 us (4%)
  starting transfers between devices  10.3 us (3%)
    all_gather x1, waiting for transfers between devices, on_device(): lax.all_gather(cotangent, 'mp', axis=2, tiled=True).reshape(count_rows, -1)  71.4 us
    all_to_all x1, waiting for transfers between devices, sum_at_owner(): lax.all_to_all(pieces, axis, split_axis=0, concat_axis=0, tiled=True)  67.1 us
    ppermute x2, waiting for transfers between devices, make_ways_on_mesh(): lax.ppermute(w_next[-1] if w_next else tile_in, axis_name=axis_key, perm=...  48.7 us
    all_gather x1, waiting for transfers between devices, on_device(): lax.all_gather(w_up, 'dp', axis=0, tiled=True)  44.3 us
    all_to_all x1, blocking collectives, sent_to_all(): return lax.all_to_all(copies, axis, split_axis=0, concat_axis=0, tiled=True)  20.2 us
    all_gather x1, waiting for transfers between devices, on_device(): lax.all_gather(inputs, 'mp', axis=2, tiled=True).reshape(count_rows, -1)  16.2 us
    dot_general x4, matrix products, gram_of(): jnp.einsum('btd,bsd->bts', cube, cube, preferred_element_type=jnp.float32)  10.8 us
    all_gather x1, local copies, waits for them, and re-layouts, on_device(): lax.all_gather(cotangent, 'mp', axis=2, tiled=True).reshape(count_rows, -1)  8.81 us
  transfers between devices with their start and end apart: 8, of which 6 were waited for; matrix products, arithmetic and copies ran while one was open for 16% of the time, Pallas kernels for 0%

profile of v1, /device:TPU:1, one launch (start us, length us, event | category | flops | bytes accessed | tf_op | source)
XLA Modules:
  0.0 390.1 jit_solution(6424586535182206242)
XLA Ops:
  13.2 24.0 %collective-permute-done = bf16[384,1536]{1,0:T(8,128)(2,1)S(1)} collective-permute-done((bf16[384,1536]{1,0:T(8,128)(2,1)}, bf16[384,1536]{1,0:T(8,128)(2,1)S(1)}, u32[]{:S(2)}, u32[]{:S(2)}) %collective-permute-start) | collective-permute-done | bytes 1179680 | tf_op jit(solution)/shard_map/ppermute | solution.py:29
  38.7 24.8 %collective-permute-done.1 = bf16[384,1536]{1,0:T(8,128)(2,1)S(1)} collective-permute-done((bf16[384,1536]{1,0:T(8,128)(2,1)S(1)}, bf16[384,1536]{1,0:T(8,128)(2,1)S(1)}, u32[]{:S(2)}, u32[]{:S(2)}) %collective-permute-start.1) | collective-permute-done | bytes 1179680 | tf_op jit(solution)/shard_map/ppermute | solution.py:29
  63.4 3.7 pad_maximum_fusion
  67.1 5.4 %gather_fusion = bf16[4,384,1536]{2,1,0:T(8,128)(2,1)} fusion(bf16[4,384,1536]{2,1,0:T(8,128)(2,1)} %pad_maximum_fusion, s32[1024]{0:T(1024)S(1)} %pad_clamp_fusion), kind=kCustom, calls=%fused_computation | custom fusion | bytes 9437200 | tf_op jit(solution)/shard_map/gather | solution.py:39
  72.5 6.8 %copy.85 = bf16[384,4,1536]{0,2,1:T(8,128)(2,1)} copy(bf16[384,4,1536]{2,0,1:T(8,128)(2,1)} %bitcast.63) | data formatting | bytes 9437184 | tf_op jit(solution)/shard_map/transpose | solution.py:12
  79.3 16.2 %all-gather.4.cloned.1.call-done = bf16[2,256,6144]{1,2,0:T(8,128)(2,1)} async-done(((bf16[2,256,96]{1,2,0:T(8,128)(2,1)}), bf16[2,256,6144]{1,2,0:T(8,128)(2,1)}) %all-gather.4.cloned.1.call-update) | async-done | bytes 6291472 | tf_op jit(solution)/shard_map/all_gather | solution.py:88
  95.5 8.7 %copy.87 = bf16[2,256,6144]{2,1,0:T(8,128)(2,1)} copy(bf16[2,256,6144]{1,2,0:T(8,128)(2,1)} %all-gather.4.cloned.1.call-done) | data formatting | bytes 12582912 | tf_op jit(solution)/shard_map/all_gather | solution.py:88
  104.2 71.4 %all-gather.6.cloned.1.call-done = bf16[2,256,6144]{1,2,0:T(8,128)(2,1)} async-done(((bf16[2,256,96]{1,2,0:T(8,128)(2,1)}), bf16[2,256,6144]{1,2,0:T(8,128)(2,1)}) %all-gather.6.cloned.1.call-update) | async-done | bytes 6291472 | tf_op jit(solution)/shard_map/all_gather | solution.py:95
  175.6 8.8 %copy.86 = bf16[2,256,6144]{2,1,0:T(8,128)(2,1)} copy(bf16[2,256,6144]{1,2,0:T(8,128)(2,1)} %all-gather.6.cloned.1.call-done) | data formatting | bytes 12582912 | tf_op jit(solution)/shard_map/all_gather | solution.py:95
  184.4 44.3 %all-gather.8.cloned.1.call-done = bf16[6144,384]{1,0:T(8,128)(2,1)} async-done(((bf16[1536,384]{1,0:T(8,128)(2,1)}), bf16[6144,384]{1,0:T(8,128)(2,1)}) %all-gather.8.cloned.1.call-update) | async-done | bytes 4718608 | tf_op jit(solution)/shard_map/all_gather | solution.py:92
  228.8 7.2 %multiply_convert_fusion.2 = (bf16[512,384]{0,1:T(8,128)(2,1)S(1)}, f32[512,384]{0,1:T(8,128)S(1)}) fusion(bf16[512,6144]{1,0:T(8,128)(2,1)} %bitcast.64, bf16[6144,384]{1,0:T(8,128)(2,1)} %all-gather.8.cloned.1.call-done), kind=kOutput, calls=%fused_computation.21 | convolution fusion | flops 2416902144 | bytes 12189696 | tf_op jit(solution)/shard_map/dot_general | solution.py:91
  236.0 2.9 fusion.2
  239.8 7.4 %fusion.3 = f32[2]{0:T(128)S(1)} fusion(f32[2,256,256]{2,1,0:T(8,128)S(1)} %fusion.9, bf16[2,256,6144]{1,2,0:T(8,128)(2,1)} %all-gather.4.cloned.1.call-done), kind=kOutput, calls=%fused_computation.14 | convolution fusion | flops 1610874880 | bytes 6815752 | tf_op jit(solution)/shard_map/btd,bsd->bts/dot_general | solution.py:82
  247.3 2.7 fusion.4
  250.1 20.2 %all_to_all.11 = f32[64,1,4]{2,1,0:T(1,128)S(1)} all-to-all(f32[64,1,4]{2,1,0:T(1,128)S(1)} %broadcast_in_dim.2), channel_id=1, replica_groups=mesh['dp'=4,'mp'=64] {'mp'}, dimensions={0} | all-to-all | bytes 2048 | tf_op jit(solution)/shard_map/all_to_all | solution.py:48
  270.5 8.6 %fusion = bf16[6144,384]{0,1:T(8,128)(2,1)} fusion(bf16[2,256,6144]{1,2,0:T(8,128)(2,1)} %all-gather.4.cloned.1.call-done, f32[2]{0:T(128)S(1)} %get-tuple-element.24, bf16[48,2,8,256]{3,2,1,0:T(8,128)(2,1)S(1)} %bitcast.77), kind=kOutput, calls=%fused_computation.5 | convolution fusion | flops 2418868224 | bytes 11403272 | tf_op jit(solution)/shard_map/dot_general | solution.py:124
  279.1 7.5 %multiply_convert_fusion = bf16[2,256,6144]{1,2,0:T(8,128)(2,1)} fusion(bf16[2,256,6144]{1,2,0:T(8,128)(2,1)} %all-gather.6.cloned.1.call-done, f32[2]{0:T(128)S(1)} %get-tuple-element.23), kind=kLoop, calls=%fused_computation.1 | loop fusion | flops 9437184 | bytes 12582920 | tf_op jit(solution)/shard_map/convert_element_type | solution.py:119
  286.6 8.7 %copy.99 = bf16[2,256,6144]{2,1,0:T(8,128)(2,1)} copy(bf16[2,256,6144]{1,2,0:T(8,128)(2,1)} %multiply_convert_fusion) | data formatting | bytes 12582912 | tf_op jit(solution)/shard_map/convert_element_type | solution.py:119
  295.3 5.6 %convolution_convert_fusion = bf16[384,6144]{1,0:T(8,128)(2,1)S(1)} fusion(bf16[512,384]{0,1:T(8,128)(2,1)S(1)} %get-tuple-element.27, bf16[512,6144]{1,0:T(8,128)(2,1)} %bitcast.66), kind=kOutput, calls=%fused_computation.4 | convolution fusion | flops 2418278400 | bytes 11403264 | tf_op jit(solution)/shard_map/dot_general | solution.py:131
  300.9 2.5 copy.119
  303.5 5.0 %all-to-all-start.1 = ((bf16[4,384,1536]{2,1,0:T(8,128)(2,1)}), bf16[4,384,1536]{2,1,0:T(8,128)(2,1)}, u32[]{:S(2)}, u32[]{:S(2)}) async-start(bf16[4,384,1536]{2,1,0:T(8,128)(2,1)} %bitcast.62), calls=%async_computation.2 | async-start | bytes 9437184 | tf_op jit(solution)/shard_map/all_to_all | solution.py:72
  309.1 67.1 %all-to-all-done.1 = bf16[4,384,1536]{2,1,0:T(8,128)(2,1)} async-done(((bf16[4,384,1536]{2,1,0:T(8,128)(2,1)}), bf16[4,384,1536]{2,1,0:T(8,128)(2,1)}, u32[]{:S(2)}, u32[]{:S(2)}) %all-to-all-start.1) | async-done | bytes 4718624 | tf_op jit(solution)/shard_map/all_to_all | solution.py:72
  376.1 4.7 %convert_reduce_fusion = f32[384,1536]{1,0:T(8,128)} fusion(bf16[4,384,1536]{2,1,0:T(8,128)(2,1)} %all-to-all-done.1), kind=kLoop, calls=%fused_computation.3 | loop fusion | flops 4128768 | bytes 7077888 | tf_op jit(solution)/shard_map/reduce_sum | solution.py:73
  380.8 2.7 copy.101
  (39 shorter events, 9.4 us)
Async XLA Ops:
  7.2 88.4 %all-gather.4.cloned.1.call-start = ((), (), s32[]{:S(2)}) async-start(), calls=%async_computation.3 | async-start | bytes 6389760 | tf_op jit(solution)/shard_map/all_gather | solution.py:88
  7.9 167.7 %all-gather.6.cloned.1.call-start = ((), (), s32[]{:S(2)}) async-start(), calls=%async_computation.4 | async-start | bytes 6389760 | tf_op jit(solution)/shard_map/all_gather | solution.py:95
  8.6 220.1 %all-gather.8.cloned.1.call-start = ((), (), s32[]{:S(2)}) async-start(), calls=%async_computation.5 | async-start | bytes 5898240 | tf_op jit(solution)/shard_map/all_gather | solution.py:92
  9.4 371.4 %reduce-scatter.2.cloned.1.call-start = ((), (), s32[]{:S(2)}) async-start(), calls=%async_computation.6 | async-start | bytes 5898240 | tf_op jit(solution)/shard_map/reduce_scatter | solution.py:123
  9.4 27.7 %collective-permute-start = (bf16[384,1536]{1,0:T(8,128)(2,1)}, bf16[384,1536]{1,0:T(8,128)(2,1)S(1)}, u32[]{:S(2)}, u32[]{:S(2)}) collective-permute-start(bf16[384,1536]{1,0:T(8,128)(2,1)} %param.8), channel_id=1, source_target_pairs={{0,64},{64,128},{128,192},{192,0},{1,65},{65,129},{129,193},{193,1... | collective-permute-start | bytes 3538952 | tf_op jit(solution)/shard_map/ppermute | solution.py:29
  11.6 27.1 %collective-permute-start.2 = (bf16[384,1536]{1,0:T(8,128)(2,1)}, bf16[384,1536]{1,0:T(8,128)(2,1)S(1)}, u32[]{:S(2)}, u32[]{:S(2)}) collective-permute-start(bf16[384,1536]{1,0:T(8,128)(2,1)} %param.8), channel_id=1, source_target_pairs={{64,0},{128,64},{192,128},{0,192},{65,1},{129,65},{193,129},{1,193... | collective-permute-start | bytes 3538952 | tf_op jit(solution)/shard_map/ppermute | solution.py:33
  37.1 26.3 %collective-permute-start.1 = (bf16[384,1536]{1,0:T(8,128)(2,1)S(1)}, bf16[384,1536]{1,0:T(8,128)(2,1)S(1)}, u32[]{:S(2)}, u32[]{:S(2)}) collective-permute-start(bf16[384,1536]{1,0:T(8,128)(2,1)S(1)} %collective-permute-done), channel_id=1, source_target_pairs={{0,64},{64,128},{128,192},{192,0},{1,65},{65,129},{129,193},{193,1... | collective-permute-start | bytes 3538952 | tf_op jit(solution)/shard_map/ppermute | solution.py:29
  175.6 60.4 %slice-start.2 = ((s8[4718592]{0:T(1024)(128)(4,1)}), s8[524288]{0:T(1024)(128)(4,1)S(1)}, s32[]{:S(2)}) async-start(s8[4718592]{0:T(1024)(128)(4,1)} %bitcast.67), calls=%async_computation.9 | async-start | bytes 1048576
  228.8 7.2 %copy-start = (bf16[2,256,6144]{2,1,0:T(8,128)(2,1)S(1)}, bf16[2,256,6144]{2,1,0:T(8,128)(2,1)}, u32[]{:S(2)}) copy-start(bf16[2,256,6144]{2,1,0:T(8,128)(2,1)} %copy.86) | copy-start | bytes 18874372
  228.8 7.2 %slice-start.3 = ((s8[4718592]{0:T(1024)(128)(4,1)}), s8[4194304]{0:T(1024)(128)(4,1)S(1)}, s32[]{:S(2)}) async-start(s8[4718592]{0:T(1024)(128)(4,1)} %bitcast.67), calls=%async_computation.10 | async-start | bytes 8388608
  239.5 7.8 %slice-start = ((s8[6291456]{0:T(1024)(128)(4,1)}), s8[4194304]{0:T(1024)(128)(4,1)S(1)}, s32[]{:S(2)}) async-start(s8[6291456]{0:T(1024)(128)(4,1)} %bitcast.60), calls=%async_computation.7 | async-start | bytes 8388608
  239.8 7.4 %slice-start.1 = ((s8[6291456]{0:T(1024)(128)(4,1)}), s8[2097152]{0:T(1024)(128)(4,1)S(1)}, s32[]{:S(2)}) async-start(s8[6291456]{0:T(1024)(128)(4,1)} %bitcast.60), calls=%async_computation.8 | async-start | bytes 4194304
  247.3 23.1 %copy-start.1 = (f32[2]{0:T(128)S(1)}, f32[2]{0:T(128)}, u32[]{:S(2)}) copy-start(f32[2]{0:T(128)} %param.9) | copy-start | bytes 28
  303.5 72.7 %all-to-all-start.1 = ((bf16[4,384,1536]{2,1,0:T(8,128)(2,1)}), bf16[4,384,1536]{2,1,0:T(8,128)(2,1)}, u32[]{:S(2)}, u32[]{:S(2)}) async-start(bf16[4,384,1536]{2,1,0:T(8,128)(2,1)} %bitcast.62), calls=%async_computation.2 | async-start | bytes 9437184 | tf_op jit(solution)/shard_map/all_to_all | solution.py:72
Sparse Core Ops, SparseCore 0:
  10.8 84.6 all-gather.3
  98.3 77.2 all-gather.5
  177.4 51.2 all-gather.7
  279.2 59.6 reduce-scatter.1
